TPU v7x, 32 devices: a whole 2x2x4 slice. The times are simulated.
32 devices in a mesh: groups: 1, row: 16 (over z, y, x), col: 2 (over core).
Axes of the slice: x: 2, y: 2, z: 4, core: 2. Of those that a mesh axis runs over, the one named last changes fastest.
Arguments:
- image: bfloat16 [64, 64, 1408], P(('groups', 'row'), None, 'col'), may hold values from -6 to 6
- kernel: float32 [7, 7, 1408], P(None, None, 'col'), may hold values from -0.875 to 0.875
- ln_gain: float32 [1408], replicated, may hold values from 0.1 to 1.9
- ln_bias: float32 [1408], replicated, may hold values from -3 to 3
- layer_scale: float32 [1408], replicated, may hold values from 0.3 to 1.5
- w_in: bfloat16 [1408, 2816], P('row', 'col'), may hold values from -0.15625 to 0.15625
- w_out: bfloat16 [2816, 1408], P('col', 'row'), may hold values from -0.109375 to 0.109375
- cotangent: bfloat16 [64, 64, 1408], P(('groups', 'row'), None, 'col'), may hold values from -16 to 16
Outputs:
- result: bfloat16 [64, 64, 1408], P(('groups', 'row'), None, 'col')
- grad_image: bfloat16 [64, 64, 1408], P(('groups', 'row'), None, 'col')
- grad_kernel: float32 [7, 7, 1408], P('groups', None, 'col')
- grad_params: float32 [3, 1408], P('groups', 'col')
All inputs are finite; a program needn't handle non-finite values.
Results may differ from a plain program's by a relative error of at most 0.0057.
Values may be sent and summed in bfloat16 or wider, within the bound.
No kernel may reach another device: no remote copies, remote signals or barrier semaphores. Data moves between devices by JAX's collectives and lax.ppermute only.
A program may use at most 64 MiB of HBM per device.

v0:
```python
import math

import jax
import jax.numpy as jnp
from jax import lax
from jax.sharding import PartitionSpec as P

epsilon = 1e-06


def padded_2(block, sides, width):
    for axis, dim in sides:
        count = lax.axis_size(axis)
        forward = [(i, i + 1) for i in range(count - 1)]
        backward = [(target, source) for source, target in forward]
        low = lax.ppermute(
            lax.slice_in_dim(block, block.shape[dim] - width, None, axis=dim), axis, forward
        )
        high = lax.ppermute(lax.slice_in_dim(block, 0, width, axis=dim), axis, backward)
        block = jnp.concatenate([low, block, high], axis=dim)
    return block


def depthwise(padded, kernel, height, breadth):
    output = jnp.zeros((height, breadth, kernel.shape[2]), jnp.float32)
    for row_tap in range(7):
        for col_tap in range(7):
            output = (
                output
                + kernel[row_tap, col_tap]
                * padded[row_tap : row_tap + height, col_tap : col_tap + breadth]
            )
    return output


def transposed(padded, kernel, height, breadth):
    output = jnp.zeros((height, breadth, kernel.shape[2]), jnp.float32)
    for row_tap in range(7):
        for col_tap in range(7):
            output = (
                output
                + kernel[row_tap, col_tap]
                * padded[6 - row_tap : 6 - row_tap + height, 6 - col_tap : 6 - col_tap + breadth]
            )
    return output


def gelu_slope(values):
    cumulative = 0.5 * (1.0 + lax.erf(values * (1.0 / math.sqrt(2.0))))
    return cumulative + values * jnp.exp(-0.5 * values * values) * (1.0 / math.sqrt(2.0 * math.pi))


def local(image, kernel, ln_gain, ln_bias, layer_scale, w_in, w_out, cotangent):
    slab_rows, grid_cols, width_part = image.shape
    tokens = slab_rows * grid_cols
    channels = ln_gain.shape[0]
    column = lax.axis_index("col")
    gain_part = lax.dynamic_slice_in_dim(ln_gain, column * width_part, width_part)
    bias_part = lax.dynamic_slice_in_dim(ln_bias, column * width_part, width_part)
    scale_part = lax.dynamic_slice_in_dim(layer_scale, column * width_part, width_part)
    extended = padded_2(image, (("row", 0),), 3)
    padded = jnp.pad(extended.astype(jnp.float32), ((0, 0), (3, 3), (0, 0)))
    conved = depthwise(padded, kernel, slab_rows, grid_cols).reshape(tokens, width_part)
    totals, squares = lax.psum((jnp.sum(conved, axis=1), jnp.sum(conved * conved, axis=1)), "col")
    average = totals / channels
    variance = squares / channels - average * average
    inv_std = lax.rsqrt(variance + epsilon)[:, None]
    normal_part = (conved - average[:, None]) * inv_std
    normed = lax.all_gather(
        (normal_part * gain_part + bias_part).astype(jnp.bfloat16), "col", axis=1, tiled=True
    )
    cot_float = cotangent.reshape(tokens, width_part).astype(jnp.float32)
    scaled = lax.all_gather(
        (cot_float * scale_part).astype(jnp.bfloat16), "col", axis=1, tiled=True
    )
    w_in_all = lax.all_gather(w_in, "row", axis=0, tiled=True)
    w_out_all = lax.all_gather(w_out, "row", axis=1, tiled=True)
    hidden = jnp.dot(normed, w_in_all, preferred_element_type=jnp.float32)
    activated = jax.nn.gelu(hidden, approximate=False).astype(jnp.bfloat16)
    branch_terms = jnp.dot(activated, w_out_all, preferred_element_type=jnp.float32)
    act_grad = jnp.einsum("tc,fc->tf", scaled, w_out_all, preferred_element_type=jnp.float32)
    branch = lax.psum_scatter(branch_terms, "col", scatter_dimension=1, tiled=True)
    result = (image.reshape(tokens, width_part).astype(jnp.float32) + scale_part * branch).astype(
        jnp.bfloat16
    )
    hid_grad = (act_grad * gelu_slope(hidden)).astype(jnp.bfloat16)
    norm_terms = jnp.einsum("tf,cf->tc", hid_grad, w_in_all, preferred_element_type=jnp.float32)
    norm_grad = lax.psum_scatter(norm_terms, "col", scatter_dimension=1, tiled=True)
    grad_hat = norm_grad * gain_part
    first_sum, second_sum = lax.psum(
        (jnp.sum(grad_hat, axis=1), jnp.sum(grad_hat * normal_part, axis=1)), "col"
    )
    conv_grad = inv_std * (
        grad_hat - first_sum[:, None] / channels - normal_part * (second_sum[:, None] / channels)
    )
    grad_field = conv_grad.reshape(slab_rows, grid_cols, width_part)
    grad_extended = padded_2(grad_field, (("row", 0),), 3)
    grad_padded = jnp.pad(grad_extended, ((0, 0), (3, 3), (0, 0)))
    grad_image = (
        cot_float.reshape(slab_rows, grid_cols, width_part)
        + transposed(grad_padded, kernel, slab_rows, grid_cols)
    ).astype(jnp.bfloat16)
    kernel_terms = jnp.stack(
        [
            jnp.stack(
                [
                    jnp.sum(
                        grad_field
                        * padded[row_tap : row_tap + slab_rows, col_tap : col_tap + grid_cols],
                        axis=(0, 1),
                    )
                    for col_tap in range(7)
                ]
            )
            for row_tap in range(7)
        ]
    )
    param_terms = jnp.stack(
        [
            jnp.sum(norm_grad * normal_part, axis=0),
            jnp.sum(norm_grad, axis=0),
            jnp.sum(cot_float * branch, axis=0),
        ]
    )
    kernel_sum, param_sum = lax.psum((kernel_terms, param_terms), "row")
    factor = 1.0 / math.sqrt(tokens * lax.axis_size("row"))
    return (
        result.reshape(slab_rows, grid_cols, width_part),
        grad_image,
        kernel_sum * factor,
        param_sum * factor,
    )


def solution(mesh):
    in_specs = (
        P(("groups", "row"), None, "col"),
        P(None, None, "col"),
        P(),
        P(),
        P(),
        P("row", "col"),
        P("col", "row"),
        P(("groups", "row"), None, "col"),
    )
    out_specs = (
        P(("groups", "row"), None, "col"),
        P(("groups", "row"), None, "col"),
        P("groups", None, "col"),
        P("groups", "col"),
    )
    return jax.shard_map(local, mesh=mesh, in_specs=in_specs, out_specs=out_specs, check_vma=False)
```

profile of v0, /device:TPU:0, one launch (start us, length us, event | category | flops | bytes accessed | tf_op | source)
XLA Modules:
  0.0 344.5 jit_solution(256962900021910612)
XLA Ops:
  7.2 0.0 all-gather.3.cloned.1.call-start
  7.3 0.7 all-gather.3.cloned.1.call-update
  7.9 0.0 all-gather.5.cloned.1.call-start
  8.0 0.7 all-gather.5.cloned.1.call-update
  8.7 0.0 reduce-scatter.3.cloned.1.call-start
  8.7 1.1 fusion.146
  9.8 4.9 %collective-permute-start = (bf16[3,64,704]{2,1,0:T(8,128)(2,1)S(1)}, bf16[3,64,704]{2,1,0:T(8,128)(2,1)S(1)}, u32[]{:S(2)}, u32[]{:S(2)}) collective-permute-start(bf16[3,64,704]{2,1,0:T(8,128)(2,1)S(1)} %get-tuple-element.122), channel_id=1, source_target_pairs={{0,2},{2,4},{4,6},{6,8},{8,10},{10,12},{12,14},{14,16},{16,18},{18... | collective-permute-start | bytes 811016 | tf_op jit(solution)/shard_map/ppermute | solution.py:16
  14.7 1.3 collective-permute-start.1
  16.0 0.1 slice_reduce_fusion.46
  16.1 0.1 dynamic_slice.10
  16.2 0.1 dynamic_slice.11
  16.3 0.2 slice_reduce_fusion.48
  16.6 0.2 slice_reduce_fusion.47
  17.0 12.0 %collective-permute-done = bf16[3,64,704]{2,1,0:T(8,128)(2,1)S(1)} collective-permute-done((bf16[3,64,704]{2,1,0:T(8,128)(2,1)S(1)}, bf16[3,64,704]{2,1,0:T(8,128)(2,1)S(1)}, u32[]{:S(2)}, u32[]{:S(2)}) %collective-permute-start) | collective-permute-done | bytes 270368 | tf_op jit(solution)/shard_map/ppermute | solution.py:16
  29.0 1.9 collective-permute-done.1
  31.0 0.2 maximum_convert_fusion
  31.5 8.2 %fusion.144 = (f32[4,64]{1,0:T(4,128)S(1)}, f32[4,64]{1,0:T(4,128)S(1)}, f32[4,64,704]{2,1,0:T(8,128)}) fusion(f32[704]{0:T(1024)S(1)} %get-tuple-element.110, f32[704]{0:T(1024)S(1)} %get-tuple-element.111, f32[704]{0:T(1024)S(1)} %get-tuple-element.64, f32[10,64,704]{2,1,0:T(8,128)S(1)} %maximum_convert_fusion, f32[704]{0:T(1024)S(1)} %get-tuple-element.65, ...), kind=kLoop, calls=%fused_computation.377 | loop fusion | flops 18021888 | bytes 8394752 | tf_op jit(solution)/shard_map/reduce_sum | solution.py:64
  39.7 0.1 reduce_sum.509
  39.8 0.1 reduce_sum.511
  39.9 1.4 copy.71
  41.3 2.5 all-reduce.3
  43.7 0.3 add_convert_fusion.1
  44.0 2.5 all_gather.12
  46.5 43.0 %all-gather.3.cloned.1.call-done = bf16[1408,1408]{1,0:T(8,128)(2,1)} async-done(((bf16[88,1408]{1,0:T(8,128)(2,1)}), bf16[1408,1408]{1,0:T(8,128)(2,1)}) %all-gather.3.cloned.1.call-update) | async-done | bytes 3964944 | tf_op jit(solution)/shard_map/all_gather | solution.py:76
  89.4 4.9 %fusion.147 = f32[256,1408]{1,0:T(8,128)} fusion(bf16[256,1408]{0,1:T(8,128)(2,1)} %all_gather.12, bf16[1408,1408]{1,0:T(8,128)(2,1)} %all-gather.3.cloned.1.call-done), kind=kOutput, calls=%fused_computation.380 | convolution fusion | flops 1015021568 | bytes 6127616 | tf_op jit(solution)/shard_map/dot_general | solution.py:78
  94.4 70.4 %all-gather.5.cloned.1.call-done = bf16[1408,1408]{0,1:T(8,128)(2,1)} async-done(((bf16[1408,88]{0,1:T(8,128)(2,1)}), bf16[1408,1408]{0,1:T(8,128)(2,1)}) %all-gather.5.cloned.1.call-update) | async-done | bytes 3964944 | tf_op jit(solution)/shard_map/all_gather | solution.py:77
  164.8 7.6 %fusion.76 = f32[256,1408]{0,1:T(8,128)} fusion(bf16[1408,1408]{0,1:T(8,128)(2,1)} %all-gather.5.cloned.1.call-done, f32[256,1408]{1,0:T(8,128)} %fusion.147), kind=kOutput, calls=%fused_computation.237 | convolution fusion | flops 1038450688 | bytes 6848512 | tf_op jit(solution)/shard_map/dot_general | solution.py:80
  172.5 0.0 reduce-scatter.5.cloned.1.call-start
  172.5 0.6 copy-done.88
  173.1 0.1 dynamic_slice.9
  173.2 1.0 bitcast_convert_fusion
  174.2 1.4 copy.72
  175.6 2.0 copy.74
  177.6 2.5 reduce-scatter.3.cloned.1.call-done
  180.1 2.3 multiply_reduce_fusion.50
  182.4 2.5 all_gather.15
  184.9 7.7 %fusion.108 = f32[256,1408]{0,1:T(8,128)} fusion(bf16[1408,1408]{1,0:T(8,128)(2,1)} %all-gather.3.cloned.1.call-done, bf16[256,1408]{0,1:T(8,128)(2,1)S(1)} %all_gather.15, bf16[1408,1408]{0,1:T(8,128)(2,1)} %all-gather.5.cloned.1.call-done, f32[256,1408]{1,0:T(8,128)} %fusion.147), kind=kOutput, calls=%fused_computation.276 | convolution fusion | flops 2033647616 | bytes 11534336 | tf_op jit(solution)/shard_map/tf,cf->tc/dot_general | solution.py:87
  192.6 0.0 all-reduce.6.cloned.1.call-start
  192.6 0.6 stack.270
  193.2 0.3 copy-done.2
  193.5 0.9 copy.73
  194.4 8.4 %reduce-scatter.5.cloned.1.call-done = f32[256,704]{0,1:T(8,128)} async-done(((f32[256,1408]{0,1:T(8,128)}), f32[256,704]{0,1:T(8,128)}) %reduce-scatter.5.cloned.1.call-update) | async-done | bytes 720912 | tf_op jit(solution)/shard_map/reduce_scatter | solution.py:88
  202.9 2.1 multiply_reduce_fusion.51
  205.0 2.4 all-reduce.2
  207.4 1.3 subtract_multiply_fusion
  208.8 0.3 copy.76
  209.0 2.3 multiply_reduce_fusion
  211.3 2.4 multiply_reduce_fusion.1
  213.7 1.1 multiply_reduce_fusion.2
  214.9 0.3 fusion.145
  215.1 0.4 copy-done.84
  216.6 0.7 copy-done.3
  217.2 0.0 all-reduce.6.cloned.1.call-update
  217.3 0.2 copy.75
  217.5 3.7 %collective-permute-start.2 = (f32[3,64,704]{2,1,0:T(8,128)S(1)}, f32[3,64,704]{2,1,0:T(8,128)S(1)}, u32[]{:S(2)}, u32[]{:S(2)}) collective-permute-start(f32[3,64,704]{2,1,0:T(8,128)S(1)} %bitcast.83), channel_id=1, source_target_pairs={{0,2},{2,4},{4,6},{6,8},{8,10},{10,12},{12,14},{14,16},{16,18},{18... | collective-permute-start | bytes 1622024 | tf_op jit(solution)/shard_map/ppermute | solution.py:16
  221.2 1.1 copy.77
  222.3 1.3 collective-permute-start.3
  223.6 93.3 %psum.47 = f32[3,704]{1,0:T(4,128)S(1)} all-reduce(f32[3,704]{1,0:T(4,128)S(1)} %pad_maximum_fusion.2), channel_id=1, replica_groups=mesh['groups'=1,'row'=16,'col'=2] {'row'}, use_global_device_ids=true, to_apply=%region_63.64 | all-reduce | flops 2112 | bytes 16896 | tf_op jit(solution)/shard_map/psum | solution.py:125
  316.9 0.6 broadcast_multiply_fusion.1
  317.5 11.2 %all-reduce.6.cloned.1.call-done = f32[7,7,704]{2,1,0:T(8,128)} async-done(((f32[7,7,704]{2,1,0:T(8,128)}), f32[7,7,704]{2,1,0:T(8,128)}) %all-reduce.6.cloned.1.call-update) | async-done | bytes 138000 | tf_op jit(solution)/shard_map/psum | solution.py:125
  328.6 1.6 broadcast_multiply_fusion
  330.6 0.2 select_maximum_fusion
  330.9 0.4 copy-done.1
  331.6 6.3 %fusion.75 = bf16[4,64,704]{2,1,0:T(8,128)(2,1)} fusion(f32[10,70,704]{2,1,0:T(8,128)S(1)} %select_maximum_fusion, f32[4,64,704]{2,1,0:T(8,128)S(1)} %bitcast.80, f32[3,64,704]{2,1,0:T(8,128)S(1)} %collective-permute-done.2, f32[3,64,704]{2,1,0:T(8,128)S(1)} %collective-permute-done.3, f32[704]{0:T(1024)S(1)} %get-tuple-element.110, f32[704]{0:T(1024)S(1)} %copy-done.6, ...), kind=kLoop, calls=%fused_computation.236 | loop fusion | flops 19103744 | bytes 32938752 | tf_op jit(solution)/shard_map/convert_element_type | solution.py:102
  (245 shorter events, 1.0 us)
Async XLA Ops:
  7.2 23.8 %copy-start = (bf16[4,64,704]{2,1,0:T(8,128)(2,1)S(1)}, bf16[4,64,704]{2,1,0:T(8,128)(2,1)}, u32[]{:S(2)}) copy-start(bf16[4,64,704]{2,1,0:T(8,128)(2,1)} %param.8) | copy-start | bytes 1081348
  7.2 8.8 %copy-start.4 = (f32[7,7,704]{2,1,0:T(8,128)S(1)}, f32[7,7,704]{2,1,0:T(8,128)}, u32[]{:S(2)}) copy-start(f32[7,7,704]{2,1,0:T(8,128)} %param.9) | copy-start | bytes 413956
  7.2 8.9 %copy-start.86 = (f32[1408]{0:T(1024)S(1)}, f32[1408]{0:T(1024)}, u32[]{:S(2)}) copy-start(f32[1408]{0:T(1024)} %param.10) | copy-start | bytes 16900
  7.2 9.0 %copy-start.87 = (f32[1408]{0:T(1024)S(1)}, f32[1408]{0:T(1024)}, u32[]{:S(2)}) copy-start(f32[1408]{0:T(1024)} %param.11) | copy-start | bytes 16900
  7.2 82.2 %all-gather.3.cloned.1.call-start = ((), (), s32[]{:S(2)}) async-start(), calls=%async_computation.2 | async-start | bytes 4212736 | tf_op jit(solution)/shard_map/all_gather | solution.py:76
  7.9 156.9 %all-gather.5.cloned.1.call-start = ((), (), s32[]{:S(2)}) async-start(), calls=%async_computation.3 | async-start | bytes 4212736 | tf_op jit(solution)/shard_map/all_gather | solution.py:77
  8.7 171.4 %reduce-scatter.3.cloned.1.call-start = ((), (), s32[]{:S(2)}) async-start(), calls=%async_computation.4 | async-start | bytes 2162688 | tf_op jit(solution)/shard_map/reduce_scatter | solution.py:82
  9.8 19.2 %collective-permute-start = (bf16[3,64,704]{2,1,0:T(8,128)(2,1)S(1)}, bf16[3,64,704]{2,1,0:T(8,128)(2,1)S(1)}, u32[]{:S(2)}, u32[]{:S(2)}) collective-permute-start(bf16[3,64,704]{2,1,0:T(8,128)(2,1)S(1)} %get-tuple-element.122), channel_id=1, source_target_pairs={{0,2},{2,4},{4,6},{6,8},{8,10},{10,12},{12,14},{14,16},{16,18},{18... | collective-permute-start | bytes 811016 | tf_op jit(solution)/shard_map/ppermute | solution.py:16
  14.7 16.3 %collective-permute-start.1 = (bf16[3,64,704]{2,1,0:T(8,128)(2,1)S(1)}, bf16[3,64,704]{2,1,0:T(8,128)(2,1)S(1)}, u32[]{:S(2)}, u32[]{:S(2)}) collective-permute-start(bf16[3,64,704]{2,1,0:T(8,128)(2,1)S(1)} %get-tuple-element.123), channel_id=1, source_target_pairs={{2,0},{4,2},{6,4},{8,6},{10,8},{12,10},{14,12},{16,14},{18,16},{20... | collective-permute-start | bytes 811016 | tf_op jit(solution)/shard_map/ppermute | solution.py:19
  16.1 15.0 %copy-start.5 = (f32[704]{0:T(1024)}, f32[704]{0:T(1024)S(1)}, u32[]{:S(2)}) copy-start(f32[704]{0:T(1024)S(1)} %get-tuple-element.111) | copy-start | bytes 8452
  16.5 14.7 %copy-start.7 = (f32[704]{0:T(1024)}, f32[704]{0:T(1024)S(1)}, u32[]{:S(2)}) copy-start(f32[704]{0:T(1024)S(1)} %get-tuple-element.63) | copy-start | bytes 8452
  16.5 14.7 %copy-start.9 = (f32[704]{0:T(1024)}, f32[704]{0:T(1024)S(1)}, u32[]{:S(2)}) copy-start(f32[704]{0:T(1024)S(1)} %get-tuple-element.64) | copy-start | bytes 8452
  16.5 14.7 %copy-start.11 = (f32[704]{0:T(1024)}, f32[704]{0:T(1024)S(1)}, u32[]{:S(2)}) copy-start(f32[704]{0:T(1024)S(1)} %get-tuple-element.65) | copy-start | bytes 8452
  16.5 14.7 %copy-start.13 = (f32[704]{0:T(1024)}, f32[704]{0:T(1024)S(1)}, u32[]{:S(2)}) copy-start(f32[704]{0:T(1024)S(1)} %get-tuple-element.66) | copy-start | bytes 8452
  16.5 14.7 %copy-start.15 = (f32[704]{0:T(1024)}, f32[704]{0:T(1024)S(1)}, u32[]{:S(2)}) copy-start(f32[704]{0:T(1024)S(1)} %get-tuple-element.67) | copy-start | bytes 8452
  16.5 14.7 %copy-start.17 = (f32[704]{0:T(1024)}, f32[704]{0:T(1024)S(1)}, u32[]{:S(2)}) copy-start(f32[704]{0:T(1024)S(1)} %get-tuple-element.68) | copy-start | bytes 8452
  16.5 14.7 %copy-start.19 = (f32[704]{0:T(1024)}, f32[704]{0:T(1024)S(1)}, u32[]{:S(2)}) copy-start(f32[704]{0:T(1024)S(1)} %get-tuple-element.69) | copy-start | bytes 8452
  16.5 14.7 %copy-start.21 = (f32[704]{0:T(1024)}, f32[704]{0:T(1024)S(1)}, u32[]{:S(2)}) copy-start(f32[704]{0:T(1024)S(1)} %get-tuple-element.70) | copy-start | bytes 8452
  16.5 14.7 %copy-start.23 = (f32[704]{0:T(1024)}, f32[704]{0:T(1024)S(1)}, u32[]{:S(2)}) copy-start(f32[704]{0:T(1024)S(1)} %get-tuple-element.71) | copy-start | bytes 8452
  16.5 14.7 %copy-start.25 = (f32[704]{0:T(1024)}, f32[704]{0:T(1024)S(1)}, u32[]{:S(2)}) copy-start(f32[704]{0:T(1024)S(1)} %get-tuple-element.72) | copy-start | bytes 8452
  16.6 14.7 %copy-start.27 = (f32[704]{0:T(1024)}, f32[704]{0:T(1024)S(1)}, u32[]{:S(2)}) copy-start(f32[704]{0:T(1024)S(1)} %get-tuple-element.73) | copy-start | bytes 8452
  16.6 14.7 %copy-start.29 = (f32[704]{0:T(1024)}, f32[704]{0:T(1024)S(1)}, u32[]{:S(2)}) copy-start(f32[704]{0:T(1024)S(1)} %get-tuple-element.74) | copy-start | bytes 8452
  16.6 14.7 %copy-start.31 = (f32[704]{0:T(1024)}, f32[704]{0:T(1024)S(1)}, u32[]{:S(2)}) copy-start(f32[704]{0:T(1024)S(1)} %get-tuple-element.75) | copy-start | bytes 8452
  16.6 14.7 %copy-start.33 = (f32[704]{0:T(1024)}, f32[704]{0:T(1024)S(1)}, u32[]{:S(2)}) copy-start(f32[704]{0:T(1024)S(1)} %get-tuple-element.76) | copy-start | bytes 8452
  16.6 14.7 %copy-start.35 = (f32[704]{0:T(1024)}, f32[704]{0:T(1024)S(1)}, u32[]{:S(2)}) copy-start(f32[704]{0:T(1024)S(1)} %get-tuple-element.77) | copy-start | bytes 8452
  16.6 14.7 %copy-start.37 = (f32[704]{0:T(1024)}, f32[704]{0:T(1024)S(1)}, u32[]{:S(2)}) copy-start(f32[704]{0:T(1024)S(1)} %get-tuple-element.78) | copy-start | bytes 8452
  16.6 14.7 %copy-start.39 = (f32[704]{0:T(1024)}, f32[704]{0:T(1024)S(1)}, u32[]{:S(2)}) copy-start(f32[704]{0:T(1024)S(1)} %get-tuple-element.79) | copy-start | bytes 8452
  16.6 14.7 %copy-start.41 = (f32[704]{0:T(1024)}, f32[704]{0:T(1024)S(1)}, u32[]{:S(2)}) copy-start(f32[704]{0:T(1024)S(1)} %get-tuple-element.80) | copy-start | bytes 8452
  16.6 14.7 %copy-start.43 = (f32[704]{0:T(1024)}, f32[704]{0:T(1024)S(1)}, u32[]{:S(2)}) copy-start(f32[704]{0:T(1024)S(1)} %get-tuple-element.81) | copy-start | bytes 8452
  16.8 14.5 %copy-start.45 = (f32[704]{0:T(1024)}, f32[704]{0:T(1024)S(1)}, u32[]{:S(2)}) copy-start(f32[704]{0:T(1024)S(1)} %get-tuple-element.82) | copy-start | bytes 8452
  16.8 14.5 %copy-start.47 = (f32[704]{0:T(1024)}, f32[704]{0:T(1024)S(1)}, u32[]{:S(2)}) copy-start(f32[704]{0:T(1024)S(1)} %get-tuple-element.83) | copy-start | bytes 8452
  16.8 14.5 %copy-start.49 = (f32[704]{0:T(1024)}, f32[704]{0:T(1024)S(1)}, u32[]{:S(2)}) copy-start(f32[704]{0:T(1024)S(1)} %get-tuple-element.84) | copy-start | bytes 8452
  16.8 14.5 %copy-start.51 = (f32[704]{0:T(1024)}, f32[704]{0:T(1024)S(1)}, u32[]{:S(2)}) copy-start(f32[704]{0:T(1024)S(1)} %get-tuple-element.85) | copy-start | bytes 8452
  16.9 14.5 %copy-start.53 = (f32[704]{0:T(1024)}, f32[704]{0:T(1024)S(1)}, u32[]{:S(2)}) copy-start(f32[704]{0:T(1024)S(1)} %get-tuple-element.86) | copy-start | bytes 8452
  16.9 14.5 %copy-start.55 = (f32[704]{0:T(1024)}, f32[704]{0:T(1024)S(1)}, u32[]{:S(2)}) copy-start(f32[704]{0:T(1024)S(1)} %get-tuple-element.87) | copy-start | bytes 8452
  16.9 14.5 %copy-start.57 = (f32[704]{0:T(1024)}, f32[704]{0:T(1024)S(1)}, u32[]{:S(2)}) copy-start(f32[704]{0:T(1024)S(1)} %get-tuple-element.88) | copy-start | bytes 8452
  16.9 14.5 %copy-start.59 = (f32[704]{0:T(1024)}, f32[704]{0:T(1024)S(1)}, u32[]{:S(2)}) copy-start(f32[704]{0:T(1024)S(1)} %get-tuple-element.89) | copy-start | bytes 8452
  16.9 14.5 %copy-start.61 = (f32[704]{0:T(1024)}, f32[704]{0:T(1024)S(1)}, u32[]{:S(2)}) copy-start(f32[704]{0:T(1024)S(1)} %get-tuple-element.90) | copy-start | bytes 8452
  16.9 14.5 %copy-start.63 = (f32[704]{0:T(1024)}, f32[704]{0:T(1024)S(1)}, u32[]{:S(2)}) copy-start(f32[704]{0:T(1024)S(1)} %get-tuple-element.91) | copy-start | bytes 8452
  16.9 14.5 %copy-start.65 = (f32[704]{0:T(1024)}, f32[704]{0:T(1024)S(1)}, u32[]{:S(2)}) copy-start(f32[704]{0:T(1024)S(1)} %get-tuple-element.92) | copy-start | bytes 8452
  16.9 14.5 %copy-start.67 = (f32[704]{0:T(1024)}, f32[704]{0:T(1024)S(1)}, u32[]{:S(2)}) copy-start(f32[704]{0:T(1024)S(1)} %get-tuple-element.93) | copy-start | bytes 8452
  16.9 14.5 %copy-start.69 = (f32[704]{0:T(1024)}, f32[704]{0:T(1024)S(1)}, u32[]{:S(2)}) copy-start(f32[704]{0:T(1024)S(1)} %get-tuple-element.94) | copy-start | bytes 8452
  16.9 14.5 %copy-start.71 = (f32[704]{0:T(1024)}, f32[704]{0:T(1024)S(1)}, u32[]{:S(2)}) copy-start(f32[704]{0:T(1024)S(1)} %get-tuple-element.95) | copy-start | bytes 8452
  17.0 14.5 %copy-start.73 = (f32[704]{0:T(1024)}, f32[704]{0:T(1024)S(1)}, u32[]{:S(2)}) copy-start(f32[704]{0:T(1024)S(1)} %get-tuple-element.96) | copy-start | bytes 8452
  17.0 14.5 %copy-start.75 = (f32[704]{0:T(1024)}, f32[704]{0:T(1024)S(1)}, u32[]{:S(2)}) copy-start(f32[704]{0:T(1024)S(1)} %get-tuple-element.97) | copy-start | bytes 8452
  17.0 14.5 %copy-start.77 = (f32[704]{0:T(1024)}, f32[704]{0:T(1024)S(1)}, u32[]{:S(2)}) copy-start(f32[704]{0:T(1024)S(1)} %get-tuple-element.98) | copy-start | bytes 8452
  17.0 14.5 %copy-start.79 = (f32[704]{0:T(1024)}, f32[704]{0:T(1024)S(1)}, u32[]{:S(2)}) copy-start(f32[704]{0:T(1024)S(1)} %get-tuple-element.99) | copy-start | bytes 8452
  17.0 14.5 %copy-start.81 = (f32[704]{0:T(1024)}, f32[704]{0:T(1024)S(1)}, u32[]{:S(2)}) copy-start(f32[704]{0:T(1024)S(1)} %get-tuple-element.100) | copy-start | bytes 8452
  172.5 30.4 %reduce-scatter.5.cloned.1.call-start = ((), (), s32[]{:S(2)}) async-start(), calls=%async_computation.5 | async-start | bytes 2162688 | tf_op jit(solution)/shard_map/reduce_scatter | solution.py:88
  192.5 1.0 copy-start.2
  192.6 136.1 %all-reduce.6.cloned.1.call-start = ((), (), s32[]{:S(2)}) async-start(), calls=%async_computation.6 | async-start | bytes 344064 | tf_op jit(solution)/shard_map/psum | solution.py:125
  216.5 7.1 %copy-start.85 = (f32[1,704]{1,0:T(1,128)S(1)}, f32[1,704]{1,0:T(1,128)}, u32[]{:S(2)}) copy-start(f32[1,704]{1,0:T(1,128)} %stack.270) | copy-start | bytes 8452
  217.5 112.7 %collective-permute-start.2 = (f32[3,64,704]{2,1,0:T(8,128)S(1)}, f32[3,64,704]{2,1,0:T(8,128)S(1)}, u32[]{:S(2)}, u32[]{:S(2)}) collective-permute-start(f32[3,64,704]{2,1,0:T(8,128)S(1)} %bitcast.83), channel_id=1, source_target_pairs={{0,2},{2,4},{4,6},{6,8},{8,10},{10,12},{12,14},{14,16},{16,18},{18... | collective-permute-start | bytes 1622024 | tf_op jit(solution)/shard_map/ppermute | solution.py:16
  222.3 108.0 %collective-permute-start.3 = (f32[3,64,704]{2,1,0:T(8,128)}, f32[3,64,704]{2,1,0:T(8,128)S(1)}, u32[]{:S(2)}, u32[]{:S(2)}) collective-permute-start(f32[3,64,704]{2,1,0:T(8,128)} %bitcast.84), channel_id=1, source_target_pairs={{2,0},{4,2},{6,4},{8,6},{10,8},{12,10},{14,12},{16,14},{18,16},{20... | collective-permute-start | bytes 1622024 | tf_op jit(solution)/shard_map/ppermute | solution.py:19
  330.3 1.0 copy-start.1
  330.3 1.0 copy-start.6
  330.3 1.0 copy-start.8
  330.3 1.0 copy-start.10
  330.3 1.0 copy-start.12
  330.3 1.0 copy-start.14
  330.3 1.0 copy-start.16
  330.3 1.0 copy-start.18
  330.3 1.0 copy-start.20
  330.3 1.0 copy-start.22
  (34 other events, 31.8 us)
Sparse Core Ops, SparseCore 0:
  10.7 78.6 all-gather.2
  92.1 72.6 all-gather.4
  172.6 7.5 reduce-scatter.2
  192.7 10.1 reduce-scatter.4
  217.4 111.2 all-reduce.5
where the time goes:
time: 345 us; the launch traced here: 344 us
  waiting for transfers between devices  151 us (44%)
  blocking collectives  103 us (30%)
  other arithmetic  29.8 us (9%)
  matrix products  20.2 us (6%)
  between operations  15.7 us (5%)
  local copies, waits for them, and re-layouts  13.4 us (4%)
  starting transfers between devices  11.3 us (3%)
    psum x1, blocking collectives, local(): kernel_sum, param_sum = lax.psum((kernel_terms, param_terms), 'row')  93.3 us
    all_gather x1, waiting for transfers between devices, local(): w_out_all = lax.all_gather(w_out, 'row', axis=1, tiled=True)  70.4 us
    all_gather x1, waiting for transfers between devices, local(): w_in_all = lax.all_gather(w_in, 'row', axis=0, tiled=True)  43 us
    ppermute x2, waiting for transfers between devices, padded_2(): lax.ppermute(lax.slice_in_dim(block, block.shape[dim] - width, None, axis...  12 us
    psum x1, waiting for transfers between devices, local(): kernel_sum, param_sum = lax.psum((kernel_terms, param_terms), 'row')  11.2 us
    ppermute x2, starting transfers between devices, padded_2(): lax.ppermute(lax.slice_in_dim(block, block.shape[dim] - width, None, axis...  8.55 us
    reduce_scatter x1, waiting for transfers between devices, local(): lax.psum_scatter(norm_terms, 'col', scatter_dimension=1, tiled=True)  8.41 us
    reduce_sum x1, other arithmetic, local(): jnp.sum(conved, axis=1)  8.17 us
  transfers between devices with their start and end apart: 9, of which 7 were waited for; matrix products, arithmetic and copies ran while one was open for 8% of the time, Pallas kernels for 0%

commit v1 on v0

v1 whole, which is shorter than its diff:
```python
import math

import jax
import jax.numpy as jnp
from jax import lax
from jax.experimental import pallas as pl
from jax.experimental.pallas import tpu as pltpu
from jax.sharding import PartitionSpec as P

epsilon = 1e-06


def exchanged(value, mask):
    count = lax.axis_size("row")
    return lax.ppermute(value, "row", [(i, i ^ mask) for i in range(count)])


def siblings(value):
    return lax.ppermute(value, "col", [(0, 1), (1, 0)])


def edges(block, width):
    count = lax.axis_size("row")
    forward = [(i, i + 1) for i in range(count - 1)]
    backward = [(i + 1, i) for i in range(count - 1)]
    low = lax.ppermute(block[block.shape[0] - width :], "row", forward)
    high = lax.ppermute(block[:width], "row", backward)
    return low, high


def gathered(shard, first, second):
    count = lax.axis_size("row")
    rows, width = shard.shape
    if count != 16:
        return lax.all_gather(shard, "row", axis=0, tiled=True)
    blocks = {0: shard}
    blocks[4] = exchanged(shard, 4)
    blocks[8] = exchanged(shard, 8)
    blocks[12] = exchanged(blocks[8], 4)
    for far in (0, 4, 8, 12):
        blocks[far + first] = exchanged(blocks[far], first)
        blocks[far + second] = exchanged(blocks[far], second)
        blocks[far + 3] = exchanged(blocks[far + first], second)
    place = lax.axis_index("row")
    whole = jnp.zeros((count * rows, width), shard.dtype)
    for mask, block in blocks.items():
        whole = lax.dynamic_update_slice(whole, block, ((place ^ mask) * rows, 0))
    return whole


def summed(value):
    count = lax.axis_size("row")
    if count & (count - 1):
        return lax.psum(value, "row")
    mask = 1
    while mask < count:
        value = value + exchanged(value, mask)
        mask *= 2
    return value


def depthwise(padded, kernel, height, breadth, flip):
    output = jnp.zeros((height, breadth, kernel.shape[2]), jnp.float32)
    for row_tap in range(7):
        for col_tap in range(7):
            row, col = (6 - row_tap, 6 - col_tap) if flip else (row_tap, col_tap)
            output = (
                output
                + kernel[row_tap, col_tap] * padded[row : row + height, col : col + breadth]
            )
    return output


def spans(extent, step):
    return [(at, min(step, extent - at)) for at in range(0, extent, step)]


def mlp_body(
    column, normed, scaled, w_in, w_out, branch_own, branch_far, norm_own, norm_far, act, grad
):
    width = w_in.shape[1]
    part = branch_own.shape[1]
    for at, size in spans(width, 256):
        lanes = slice(at, at + size)
        hidden = jnp.dot(normed[...], w_in[:, lanes], preferred_element_type=jnp.float32)
        act_grad = jnp.dot(scaled[...], w_out[:, lanes], preferred_element_type=jnp.float32)
        cumulative = 0.5 * (1.0 + lax.erf(hidden * (1.0 / math.sqrt(2.0))))
        slope = cumulative + hidden * jnp.exp(-0.5 * hidden * hidden) * (
            1.0 / math.sqrt(2.0 * math.pi)
        )
        act[:, lanes] = (hidden * cumulative).astype(jnp.bfloat16)
        grad[:, lanes] = (act_grad * slope).astype(jnp.bfloat16)
    own = pl.multiple_of(column[0] * part, part)
    far = pl.multiple_of((1 - column[0]) * part, part)
    contract = (((1,), (1,)), ((), ()))
    for left, weights, outs in (
        (grad, w_in, ((norm_far, far), (norm_own, own))),
        (act, w_out, ((branch_far, far), (branch_own, own))),
    ):
        for out, start in outs:
            for at, size in spans(part, 256):
                out[:, at : at + size] = lax.dot_general(
                    left[...],
                    weights[pl.ds(start + at, size), :],
                    contract,
                    preferred_element_type=jnp.float32,
                )


def mlp(column, normed, scaled, w_in, w_out):
    tokens, channels = normed.shape
    width = w_in.shape[1]
    part = jax.ShapeDtypeStruct((tokens, channels // 2), jnp.float32)
    return pl.pallas_call(
        mlp_body,
        out_shape=(part,) * 4,
        in_specs=[pl.BlockSpec(memory_space=pltpu.SMEM)]
        + [pl.BlockSpec(memory_space=pltpu.VMEM)] * 4,
        out_specs=(pl.BlockSpec(memory_space=pltpu.VMEM),) * 4,
        scratch_shapes=[pltpu.VMEM((tokens, width), jnp.bfloat16)] * 2,
        compiler_params=pltpu.CompilerParams(vmem_limit_bytes=32 << 20),
        cost_estimate=pl.CostEstimate(
            flops=8 * tokens * channels * width,
            bytes_accessed=4 * channels * width + 16 * tokens * channels,
            transcendentals=2 * tokens * width,
        ),
        name="mlp",
    )(column.reshape(1), normed, scaled, w_in, w_out)


def local(image, kernel, ln_gain, ln_bias, layer_scale, w_in, w_out, cotangent):
    slab_rows, grid_cols, width_part = image.shape
    tokens = slab_rows * grid_cols
    channels = ln_gain.shape[0]
    column = lax.axis_index("col").astype(jnp.int32)
    gain_part = lax.dynamic_slice_in_dim(ln_gain, column * width_part, width_part)
    bias_part = lax.dynamic_slice_in_dim(ln_bias, column * width_part, width_part)
    scale_part = lax.dynamic_slice_in_dim(layer_scale, column * width_part, width_part)
    low, high = edges(image, 3)
    w_in_all = gathered(w_in, 2, 1)
    w_out_all = gathered(w_out.T, 1, 2)
    extended = jnp.concatenate([low, image, high], axis=0)
    padded = jnp.pad(extended.astype(jnp.float32), ((0, 0), (3, 3), (0, 0)))
    conved = depthwise(padded, kernel, slab_rows, grid_cols, False).reshape(tokens, width_part)
    totals, squares = lax.psum((jnp.sum(conved, axis=1), jnp.sum(conved * conved, axis=1)), "col")
    average = totals / channels
    variance = squares / channels - average * average
    inv_std = lax.rsqrt(variance + epsilon)[:, None]
    normal_part = (conved - average[:, None]) * inv_std
    normed = lax.all_gather(
        (normal_part * gain_part + bias_part).astype(jnp.bfloat16), "col", axis=1, tiled=True
    )
    cot_float = cotangent.reshape(tokens, width_part).astype(jnp.float32)
    scaled = lax.all_gather(
        (cot_float * scale_part).astype(jnp.bfloat16), "col", axis=1, tiled=True
    )
    branch_own, branch_far, norm_own, norm_far = mlp(column, normed, scaled, w_in_all, w_out_all)
    norm_grad = norm_own + siblings(norm_far)
    branch = branch_own + siblings(branch_far)
    result = (image.reshape(tokens, width_part).astype(jnp.float32) + scale_part * branch).astype(
        jnp.bfloat16
    )
    grad_hat = norm_grad * gain_part
    first_sum, second_sum = lax.psum(
        (jnp.sum(grad_hat, axis=1), jnp.sum(grad_hat * normal_part, axis=1)), "col"
    )
    conv_grad = inv_std * (
        grad_hat - first_sum[:, None] / channels - normal_part * (second_sum[:, None] / channels)
    )
    grad_field = conv_grad.reshape(slab_rows, grid_cols, width_part)
    low, high = edges(grad_field.astype(jnp.bfloat16), 3)
    grad_extended = jnp.concatenate(
        [low.astype(jnp.float32), grad_field, high.astype(jnp.float32)], axis=0
    )
    grad_padded = jnp.pad(grad_extended, ((0, 0), (3, 3), (0, 0)))
    grad_image = (
        cot_float.reshape(slab_rows, grid_cols, width_part)
        + depthwise(grad_padded, kernel, slab_rows, grid_cols, True)
    ).astype(jnp.bfloat16)
    terms = [
        jnp.sum(
            grad_field * padded[row_tap : row_tap + slab_rows, col_tap : col_tap + grid_cols],
            axis=(0, 1),
        )
        for row_tap in range(7)
        for col_tap in range(7)
    ]
    terms += [
        jnp.sum(norm_grad * normal_part, axis=0),
        jnp.sum(norm_grad, axis=0),
        jnp.sum(cot_float * branch, axis=0),
    ]
    factor = 1.0 / math.sqrt(tokens * lax.axis_size("row"))
    sums = summed(jnp.stack(terms)) * factor
    return (
        result.reshape(slab_rows, grid_cols, width_part),
        grad_image,
        sums[:49].reshape(7, 7, width_part),
        sums[49:],
    )


def solution(mesh):
    in_specs = (
        P(("groups", "row"), None, "col"),
        P(None, None, "col"),
        P(),
        P(),
        P(),
        P("row", "col"),
        P("col", "row"),
        P(("groups", "row"), None, "col"),
    )
    out_specs = (
        P(("groups", "row"), None, "col"),
        P(("groups", "row"), None, "col"),
        P("groups", None, "col"),
        P("groups", "col"),
    )
    return jax.shard_map(local, mesh=mesh, in_specs=in_specs, out_specs=out_specs, check_vma=False)
```

time: 345 us -> 208 us (0.60)
  waiting for transfers between devices: 151 us -> 49.5 us
  blocking collectives: 103 us -> 10.1 us
  starting transfers between devices: 11.3 us -> 54.5 us
  local copies, waits for them, and re-layouts: 13.4 us -> 53.9 us
  matrix products: 20.2 us -> 0 us
  between operations: 15.7 us -> 2.93 us
  Pallas kernels: 0 us -> 8.39 us
    all_gather x2 -> x0, waiting for transfers between devices: 113 us -> none  [the longest x1 70.4 us: local(): w_out_all = lax.all_gather(w_out, 'row', axis=1, tiled=True)]
    psum x1 -> x0, blocking collectives: 93.3 us -> none  [local(): kernel_sum, param_sum = lax.psum((kernel_terms, param_terms), 'row')]
    ppermute x4 -> x40, starting transfers between devices: 11.1 us -> 54.5 us  [the longest x34 45.9 us: exchanged(): return lax.ppermute(value, 'row', [(i, i ^ mask) for i in range(count)])]
    ppermute x4 -> x40, waiting for transfers between devices: 14 us -> 49.5 us  [the longest x34 36.3 us: exchanged(): return lax.ppermute(value, 'row', [(i, i ^ mask) for i in range(count)])]
    dynamic_update_slice x0 -> x32, local copies, waits for them, and re-layouts: none -> 26.7 us  [gathered(): whole = lax.dynamic_update_slice(whole, block, ((place ^ mask) * rows, 0))]
    dot_general x3 -> x0, matrix products: 20.2 us -> none  [the longest x1 7.65 us: local(): jnp.einsum('tf,cf->tc', hid_grad, w_in_all, preferred_element_type=jnp.fl...]
    another operation x60 -> x55, local copies, waits for them, and re-layouts: 1.13 us -> 15.4 us  [the longest x53 11.1 us: local(): sums = summed(jnp.stack(terms)) * factor]
    psum x1 -> x0, waiting for transfers between devices: 11.2 us -> none  [local(): kernel_sum, param_sum = lax.psum((kernel_terms, param_terms), 'row')]
  transfers between devices with their start and end apart: 9 -> 40, of which waited for: 7 -> 15; matrix products, arithmetic and copies ran while one was open for 8% -> 36% of each run, Pallas kernels for 0% -> 0%
where the time goes in v1:
time: 208 us; the launch traced here: 207 us
  starting transfers between devices  54.5 us (26%)
  local copies, waits for them, and re-layouts  53.9 us (26%)
  waiting for transfers between devices  49.5 us (24%)
  other arithmetic  28 us (13%)
  blocking collectives  10.1 us (5%)
  Pallas kernels  8.39 us (4%)
  between operations  2.93 us (1%)
    ppermute x34, starting transfers between devices, exchanged(): return lax.ppermute(value, 'row', [(i, i ^ mask) for i in range(count)])  45.9 us
    ppermute x34, waiting for transfers between devices, exchanged(): return lax.ppermute(value, 'row', [(i, i ^ mask) for i in range(count)])  36.3 us
    dynamic_update_slice x32, local copies, waits for them, and re-layouts, gathered(): whole = lax.dynamic_update_slice(whole, block, ((place ^ mask) * rows, 0))  26.7 us
    another operation x53, local copies, waits for them, and re-layouts, local(): sums = summed(jnp.stack(terms)) * factor  11.1 us
    pallas_call x1, Pallas kernels, mlp(): pl.pallas_call(mlp_body, out_shape=(part,) * 4, in_specs=[pl.BlockSpec(me...  8.39 us
    reduce_sum x1, other arithmetic, local(): jnp.sum(conved, axis=1)  7.58 us
    convert_element_type x1, other arithmetic, local(): grad_image = (cot_float.reshape(slab_rows, grid_cols, width_part) + depth...  7.2 us
    reduce_sum x3, other arithmetic, local(): jnp.sum(grad_field * padded[row_tap:row_tap + slab_rows, col_tap:col_tap...  7.12 us
  transfers between devices with their start and end apart: 40, of which 15 were waited for; matrix products, arithmetic and copies ran while one was open for 36% of the time, Pallas kernels for 0%

profile of v1, /device:TPU:0, one launch (start us, length us, event | category | flops | bytes accessed | tf_op | source)
XLA Modules:
  0.0 207.3 jit_solution(18280347023090289754)
XLA Ops:
  0.6 3.1 %collective-permute-start.17 = (bf16[88,1408]{1,0:T(8,128)(2,1)}, bf16[88,1408]{1,0:T(8,128)(2,1)S(1)}, u32[]{:S(2)}, u32[]{:S(2)}) collective-permute-start(bf16[88,1408]{1,0:T(8,128)(2,1)} %bitcast.83), channel_id=1, source_target_pairs={{0,8},{2,10},{4,12},{6,14},{8,0},{10,2},{12,4},{14,6},{16,24},{18,... | collective-permute-start | bytes 743432 | tf_op jit(solution)/shard_map/ppermute | solution.py:15
  3.7 2.6 %collective-permute-start.18 = (bf16[88,1408]{1,0:T(8,128)(2,1)}, bf16[88,1408]{1,0:T(8,128)(2,1)S(1)}, u32[]{:S(2)}, u32[]{:S(2)}) collective-permute-start(bf16[88,1408]{1,0:T(8,128)(2,1)} %bitcast.84), channel_id=1, source_target_pairs={{0,16},{2,18},{4,20},{6,22},{8,24},{10,26},{12,28},{14,30},{16,0},... | collective-permute-start | bytes 743432 | tf_op jit(solution)/shard_map/ppermute | solution.py:15
  6.3 1.5 collective-permute-start.20
  7.8 1.5 collective-permute-start.21
  9.8 2.2 %broadcast.25.clone.1 = bf16[1408,1408]{1,0:T(8,128)(2,1)} broadcast(bf16[]{:T(256)} %constant.13.clone.1), dimensions={} | broadcast | bytes 3964930 | tf_op jit(solution)/shard_map/broadcast.5
  12.7 2.2 %broadcast.25.clone = bf16[1408,1408]{1,0:T(8,128)(2,1)} broadcast(bf16[]{:T(256)} %constant.13.clone.1), dimensions={} | broadcast | bytes 3964930 | tf_op jit(solution)/shard_map/broadcast.5
  15.6 0.7 slice_reduce_fusion.47
  16.9 2.3 %all_gather.7 = bf16[256,1408]{0,1:T(8,128)(2,1)S(1)} all-gather(bf16[256,704]{0,1:T(8,128)(2,1)S(1)} %copy.13), channel_id=1, replica_groups=mesh['groups'=1,'row'=16,'col'=2] {'col'}, dimensions={1}, use_global_device_ids=true | all-gather | bytes 1081344 | tf_op jit(solution)/shard_map/all_gather | solution.py:154
  20.0 1.1 copy.15.scaled
  22.3 2.4 %collective-permute-start = (bf16[3,64,704]{2,1,0:T(8,128)(2,1)S(1)}, bf16[3,64,704]{2,1,0:T(8,128)(2,1)S(1)}, u32[]{:S(2)}, u32[]{:S(2)}) collective-permute-start(bf16[3,64,704]{2,1,0:T(8,128)(2,1)S(1)} %get-tuple-element.127), channel_id=1, source_target_pairs={{0,2},{2,4},{4,6},{6,8},{8,10},{10,12},{12,14},{14,16},{16,18},{18... | collective-permute-start | bytes 811016 | tf_op jit(solution)/shard_map/ppermute | solution.py:26
  25.4 1.3 collective-permute-start.1
  26.7 0.7 constant_dynamic-update-slice_fusion.13
  27.4 8.8 %collective-permute-done.3 = bf16[88,1408]{1,0:T(8,128)(2,1)S(1)} collective-permute-done((bf16[88,1408]{1,0:T(8,128)(2,1)S(1)}, bf16[88,1408]{1,0:T(8,128)(2,1)S(1)}, u32[]{:S(2)}, u32[]{:S(2)}) %collective-permute-start.3) | collective-permute-done | bytes 247840 | tf_op jit(solution)/shard_map/ppermute | solution.py:15
  37.2 2.8 %collective-permute-done.1 = bf16[3,64,704]{2,1,0:T(8,128)(2,1)S(1)} collective-permute-done((bf16[3,64,704]{2,1,0:T(8,128)(2,1)S(1)}, bf16[3,64,704]{2,1,0:T(8,128)(2,1)S(1)}, u32[]{:S(2)}, u32[]{:S(2)}) %collective-permute-start.1) | collective-permute-done | bytes 270368 | tf_op jit(solution)/shard_map/ppermute | solution.py:27
  40.0 1.9 collective-permute-start.19
  42.2 7.6 %fusion.65 = (f32[4,64]{1,0:T(4,128)S(1)}, f32[4,64]{1,0:T(4,128)S(1)}, f32[4,64,704]{2,1,0:T(8,128)S(1)}) fusion(f32[704]{0:T(1024)S(1)} %get-tuple-element.114, f32[704]{0:T(1024)S(1)} %get-tuple-element.115, f32[704]{0:T(1024)S(1)} %get-tuple-element.68, f32[10,64,704]{2,1,0:T(8,128)S(1)} %maximum_convert_fusion, f32[704]{0:T(1024)S(1)} %get-tuple-element.69, ...), kind=kLoop, calls=%fused_computation.310 | loop fusion | flops 18021888 | bytes 8394752 | tf_op jit(solution)/shard_map/reduce_sum | solution.py:145
  50.3 2.4 %all-reduce.3 = (f32[256]{0:T(256)S(1)}, f32[256]{0:T(256)S(1)}) all-reduce(f32[256]{0:T(256)S(1)} %reduce_sum.511, f32[256]{0:T(256)S(1)} %reduce_sum.509), channel_id=1, replica_groups=mesh['groups'=1,'row'=16,'col'=2] {'col'}, use_global_device_ids=true, to_apply=%region_3.4 | all-reduce | flops 512 | bytes 4096 | tf_op jit(solution)/shard_map/psum | solution.py:145
  53.1 2.5 %all_gather.6 = bf16[256,1408]{0,1:T(8,128)(2,1)S(1)} all-gather(bf16[256,704]{0,1:T(8,128)(2,1)S(1)} %copy.12), channel_id=1, replica_groups=mesh['groups'=1,'row'=16,'col'=2] {'col'}, dimensions={1}, use_global_device_ids=true | all-gather | bytes 1081344 | tf_op jit(solution)/shard_map/all_gather | solution.py:150
  55.6 1.1 copy.14.normed
  56.9 1.3 collective-permute-start.22
  58.9 1.6 constant_dynamic-update-slice_fusion.11
  60.6 4.2 %collective-permute-done.4 = bf16[88,1408]{1,0:T(8,128)(2,1)S(1)} collective-permute-done((bf16[88,1408]{1,0:T(8,128)(2,1)S(1)}, bf16[88,1408]{1,0:T(8,128)(2,1)S(1)}, u32[]{:S(2)}, u32[]{:S(2)}) %collective-permute-start.4) | collective-permute-done | bytes 247840 | tf_op jit(solution)/shard_map/ppermute | solution.py:15
  64.8 0.7 constant_dynamic-update-slice_fusion.28
  65.6 3.5 %collective-permute-start.24 = (bf16[88,1408]{1,0:T(8,128)(2,1)S(1)}, bf16[88,1408]{1,0:T(8,128)(2,1)S(1)}, u32[]{:S(2)}, u32[]{:S(2)}) collective-permute-start(bf16[88,1408]{1,0:T(8,128)(2,1)S(1)} %collective-permute-done.17), channel_id=1, source_target_pairs={{0,4},{2,6},{4,0},{6,2},{8,12},{10,14},{12,8},{14,10},{16,20},{18,... | collective-permute-start | bytes 743432 | tf_op jit(solution)/shard_map/ppermute | solution.py:15
  69.1 1.7 constant_dynamic-update-slice_fusion.10
  70.8 1.7 constant_dynamic-update-slice_fusion.27
  72.4 2.0 collective-permute-start.7
  74.5 1.7 constant_dynamic-update-slice_fusion.26
  76.9 5.9 %collective-permute-done.7 = bf16[88,1408]{1,0:T(8,128)(2,1)S(1)} collective-permute-done((bf16[88,1408]{1,0:T(8,128)(2,1)}, bf16[88,1408]{1,0:T(8,128)(2,1)S(1)}, u32[]{:S(2)}, u32[]{:S(2)}) %collective-permute-start.7) | collective-permute-done | bytes 247840 | tf_op jit(solution)/shard_map/ppermute | solution.py:15
  82.8 1.7 collective-permute-start.8
  85.2 1.7 collective-permute-start.9
  88.4 2.5 %collective-permute-done.8 = bf16[88,1408]{1,0:T(8,128)(2,1)S(1)} collective-permute-done((bf16[88,1408]{1,0:T(8,128)(2,1)S(1)}, bf16[88,1408]{1,0:T(8,128)(2,1)S(1)}, u32[]{:S(2)}, u32[]{:S(2)}) %collective-permute-start.8) | collective-permute-done | bytes 247840 | tf_op jit(solution)/shard_map/ppermute | solution.py:15
  91.0 2.5 %collective-permute-start.25 = (bf16[88,1408]{1,0:T(8,128)(2,1)S(1)}, bf16[88,1408]{1,0:T(8,128)(2,1)S(1)}, u32[]{:S(2)}, u32[]{:S(2)}) collective-permute-start(bf16[88,1408]{1,0:T(8,128)(2,1)S(1)} %collective-permute-done.23), channel_id=1, source_target_pairs={{0,4},{2,6},{4,0},{6,2},{8,12},{10,14},{12,8},{14,10},{16,20},{18,... | collective-permute-start | bytes 743432 | tf_op jit(solution)/shard_map/ppermute | solution.py:15
  94.2 1.7 collective-permute-start.12
  96.9 3.1 %collective-permute-done.25 = bf16[88,1408]{1,0:T(8,128)(2,1)S(1)} collective-permute-done((bf16[88,1408]{1,0:T(8,128)(2,1)S(1)}, bf16[88,1408]{1,0:T(8,128)(2,1)S(1)}, u32[]{:S(2)}, u32[]{:S(2)}) %collective-permute-start.25) | collective-permute-done | bytes 247840 | tf_op jit(solution)/shard_map/ppermute | solution.py:15
  100.0 1.7 collective-permute-start.28
  103.2 1.8 collective-permute-start.29
  107.9 2.5 %collective-permute-start.14 = (bf16[88,1408]{1,0:T(8,128)(2,1)S(1)}, bf16[88,1408]{1,0:T(8,128)(2,1)S(1)}, u32[]{:S(2)}, u32[]{:S(2)}) collective-permute-start(bf16[88,1408]{1,0:T(8,128)(2,1)S(1)} %collective-permute-done.4), channel_id=1, source_target_pairs={{0,4},{2,6},{4,0},{6,2},{8,12},{10,14},{12,8},{14,10},{16,20},{18,... | collective-permute-start | bytes 743432 | tf_op jit(solution)/shard_map/ppermute | solution.py:15
  111.1 0.9 collective-permute-done.29
  112.0 2.0 collective-permute-start.15
  114.7 4.8 %collective-permute-done.14 = bf16[88,1408]{1,0:T(8,128)(2,1)S(1)} collective-permute-done((bf16[88,1408]{1,0:T(8,128)(2,1)S(1)}, bf16[88,1408]{1,0:T(8,128)(2,1)S(1)}, u32[]{:S(2)}, u32[]{:S(2)}) %collective-permute-start.14) | collective-permute-done | bytes 247840 | tf_op jit(solution)/shard_map/ppermute | solution.py:15
  124.5 1.2 collective-permute-done.16
  126.4 8.4 %mlp.1 = (f32[256,704]{1,0:T(8,128)S(1)}, f32[256,704]{1,0:T(8,128)S(1)}, f32[256,704]{1,0:T(8,128)S(1)}, f32[256,704]{1,0:T(8,128)S(1)}) custom-call(s32[1]{0:T(128)} %bitcast.1.column, bf16[256,1408]{1,0:T(8,128)(2,1)S(1)} %copy-done.1, bf16[256,1408]{1,0:T(8,128)(2,1)S(1)} %copy-done, bf16[1408,1408]{1,0:T(8,128)(2,1)} %constant_dynamic-update-slice_fusion.16.w_in, ...), custom_call_target="tpu_custom_call" | custom-call | flops 4060086272 | bytes 13697024 | tf_op jit(solution)/shard_map/mlp/pallas_call | solution.py:114
  134.8 1.1 copy.18
  135.9 1.1 copy.16
  137.6 0.9 collective-permute-done.33
  138.5 2.3 %copy.19 = f32[256,704]{1,0:T(8,128)} copy(f32[256,704]{0,1:T(8,128)} %collective-permute-done.33) | data formatting | bytes 1441792 | tf_op jit(solution)/shard_map/ppermute | solution.py:19
  140.7 3.2 %multiply_reduce_fusion = (f32[704]{0:T(1024)}, f32[256]{0:T(256)}, f32[256]{0:T(256)}, f32[704]{0:T(1024)}, f32[256,704]{1,0:T(8,128)}) fusion(f32[4,64,704]{2,1,0:T(8,128)} %copy-done.4, f32[256]{0:T(256)S(1)} %get-tuple-element.130, f32[256]{0:T(256)S(1)} %get-tuple-element.129, f32[704]{0:T(1024)S(1)} %dynamic_slice.10, ...), kind=kLoop, calls=%fused_computation.167 | loop fusion | flops 1800320 | bytes 2896128 | tf_op jit(solution)/shard_map/reduce_sum | solution.py:189
  143.9 2.8 %all-reduce.2 = (f32[256]{0:T(256)S(1)}, f32[256]{0:T(256)S(1)}) all-reduce(f32[256]{0:T(256)} %get-tuple-element.62, f32[256]{0:T(256)} %get-tuple-element.63), channel_id=1, replica_groups=mesh['groups'=1,'row'=16,'col'=2] {'col'}, use_global_device_ids=true, to_apply=%region_7.8 | all-reduce | flops 512 | bytes 4096 | tf_op jit(solution)/shard_map/psum | solution.py:164
  146.7 3.7 %multiply_reduce_fusion.2 = (f32[704]{0:T(1024)S(1)}, f32[704]{0:T(1024)S(1)}, f32[704]{0:T(1024)S(1)}, f32[704]{0:T(1024)S(1)}, f32[704]{0:T(1024)S(1)}, /*inde...) fusion(f32[10,64,704]{2,1,0:T(8,128)S(1)} %copy-done.3, ...), kind=kLoop, calls=%fused_computation.169 | loop fusion | flops 7736960 | bytes 4022528 | tf_op jit(solution)/shard_map/reduce_sum | solution.py:181
  150.4 2.3 %multiply_reduce_fusion.1 = (f32[704]{0:T(1024)S(1)}, f32[704]{0:T(1024)S(1)}, f32[704]{0:T(1024)S(1)}, f32[704]{0:T(1024)S(1)}, f32[704]{0:T(1024)S(1)}, /*inde...) fusion(f32[10,64,704]{2,1,0:T(8,128)S(1)} %copy-done.3, ...), kind=kLoop, calls=%fused_computation.168 | loop fusion | flops 6475392 | bytes 3589632 | tf_op jit(solution)/shard_map/reduce_sum | solution.py:181
  163.3 1.1 multiply_reduce_fusion.3
  165.0 1.4 copy.17
  166.4 2.1 fusion.62
  169.0 0.8 collective-permute-start.36
  170.3 3.2 %collective-permute-start.34 = (bf16[3,64,704]{2,1,0:T(8,128)(2,1)S(1)}, bf16[3,64,704]{2,1,0:T(8,128)(2,1)S(1)}, u32[]{:S(2)}, u32[]{:S(2)}) collective-permute-start(bf16[3,64,704]{2,1,0:T(8,128)(2,1)S(1)} %get-tuple-element.125), channel_id=1, source_target_pairs={{0,2},{2,4},{4,6},{6,8},{8,10},{10,12},{12,14},{14,16},{16,18},{18... | collective-permute-start | bytes 811016 | tf_op jit(solution)/shard_map/ppermute | solution.py:26
  173.5 1.3 collective-permute-start.35
  175.5 3.8 %collective-permute-start.37 = (f32[52,704]{1,0:T(8,128)S(1)}, f32[52,704]{1,0:T(8,128)S(1)}, u32[]{:S(2)}, u32[]{:S(2)}) collective-permute-start(f32[52,704]{1,0:T(8,128)S(1)} %add.528), channel_id=1, source_target_pairs={{0,4},{2,6},{4,0},{6,2},{8,12},{10,14},{12,8},{14,10},{16,20},{18,... | collective-permute-start | bytes 439304 | tf_op jit(solution)/shard_map/ppermute | solution.py:15
  179.3 7.1 %collective-permute-done.34 = bf16[3,64,704]{2,1,0:T(8,128)(2,1)S(1)} collective-permute-done((bf16[3,64,704]{2,1,0:T(8,128)(2,1)S(1)}, bf16[3,64,704]{2,1,0:T(8,128)(2,1)S(1)}, u32[]{:S(2)}, u32[]{:S(2)}) %collective-permute-start.34) | collective-permute-done | bytes 270368 | tf_op jit(solution)/shard_map/ppermute | solution.py:26
  186.4 2.5 %collective-permute-done.35 = bf16[3,64,704]{2,1,0:T(8,128)(2,1)S(1)} collective-permute-done((bf16[3,64,704]{2,1,0:T(8,128)(2,1)S(1)}, bf16[3,64,704]{2,1,0:T(8,128)(2,1)S(1)}, u32[]{:S(2)}, u32[]{:S(2)}) %collective-permute-start.35) | collective-permute-done | bytes 270368 | tf_op jit(solution)/shard_map/ppermute | solution.py:27
  189.0 1.5 collective-permute-start.38
  190.7 3.8 %collective-permute-done.38 = f32[52,704]{1,0:T(8,128)S(1)} collective-permute-done((f32[52,704]{1,0:T(8,128)S(1)}, f32[52,704]{1,0:T(8,128)S(1)}, u32[]{:S(2)}, u32[]{:S(2)}) %collective-permute-start.38) | collective-permute-done | bytes 146464 | tf_op jit(solution)/shard_map/ppermute | solution.py:15
  194.5 3.9 %collective-permute-start.39 = (f32[52,704]{1,0:T(8,128)S(1)}, f32[52,704]{1,0:T(8,128)S(1)}, u32[]{:S(2)}, u32[]{:S(2)}) collective-permute-start(f32[52,704]{1,0:T(8,128)S(1)} %add.530), channel_id=1, source_target_pairs={{0,16},{2,18},{4,20},{6,22},{8,24},{10,26},{12,28},{14,30},{16,0},... | collective-permute-start | bytes 439304 | tf_op jit(solution)/shard_map/ppermute | solution.py:15
  198.8 7.2 %fusion.64 = bf16[4,64,704]{2,1,0:T(8,128)(2,1)} fusion(f32[10,70,704]{2,1,0:T(8,128)S(1)} %select_maximum_fusion, f32[4,64,704]{2,1,0:T(8,128)S(1)} %bitcast.80, f32[3,64,704]{2,1,0:T(8,128)S(1)} %convert_element_type.52, f32[3,64,704]{2,1,0:T(8,128)S(1)} %convert_element_type.53, bf16[4,64,704]{2,1,0:T(8,128)(2,1)S(1)} %copy-done.7, f32[704]{0:T(1024)} %copy-done.96, ...), kind=kLoop, calls=%fused_computation.222 | loop fusion | flops 19103744 | bytes 32938752 | tf_op jit(solution)/shard_map/convert_element_type | solution.py:179
  (394 shorter events, 37.6 us)
Async XLA Ops:
  0.6 20.5 %collective-permute-start.17 = (bf16[88,1408]{1,0:T(8,128)(2,1)}, bf16[88,1408]{1,0:T(8,128)(2,1)S(1)}, u32[]{:S(2)}, u32[]{:S(2)}) collective-permute-start(bf16[88,1408]{1,0:T(8,128)(2,1)} %bitcast.83), channel_id=1, source_target_pairs={{0,8},{2,10},{4,12},{6,14},{8,0},{10,2},{12,4},{14,6},{16,24},{18,... | collective-permute-start | bytes 743432 | tf_op jit(solution)/shard_map/ppermute | solution.py:15
  3.7 21.7 %collective-permute-start.18 = (bf16[88,1408]{1,0:T(8,128)(2,1)}, bf16[88,1408]{1,0:T(8,128)(2,1)S(1)}, u32[]{:S(2)}, u32[]{:S(2)}) collective-permute-start(bf16[88,1408]{1,0:T(8,128)(2,1)} %bitcast.84), channel_id=1, source_target_pairs={{0,16},{2,18},{4,20},{6,22},{8,24},{10,26},{12,28},{14,30},{16,0},... | collective-permute-start | bytes 743432 | tf_op jit(solution)/shard_map/ppermute | solution.py:15
  6.3 50.4 %collective-permute-start.20 = (bf16[88,1408]{1,0:T(8,128)(2,1)}, bf16[88,1408]{1,0:T(8,128)(2,1)}, u32[]{:S(2)}, u32[]{:S(2)}) collective-permute-start(bf16[88,1408]{1,0:T(8,128)(2,1)} %bitcast.85), channel_id=1, source_target_pairs={{0,2},{2,0},{4,6},{6,4},{8,10},{10,8},{12,14},{14,12},{16,18},{18,... | collective-permute-start | bytes 743432 | tf_op jit(solution)/shard_map/ppermute | solution.py:15
  7.8 57.8 %collective-permute-start.21 = (bf16[88,1408]{1,0:T(8,128)(2,1)}, bf16[88,1408]{1,0:T(8,128)(2,1)}, u32[]{:S(2)}, u32[]{:S(2)}) collective-permute-start(bf16[88,1408]{1,0:T(8,128)(2,1)} %bitcast.86), channel_id=1, source_target_pairs={{0,4},{2,6},{4,0},{6,2},{8,12},{10,14},{12,8},{14,10},{16,20},{18,... | collective-permute-start | bytes 743432 | tf_op jit(solution)/shard_map/ppermute | solution.py:15
  9.3 12.9 %collective-permute-start.2 = (bf16[88,1408]{1,0:T(8,128)(2,1)}, bf16[88,1408]{1,0:T(8,128)(2,1)S(1)}, u32[]{:S(2)}, u32[]{:S(2)}) collective-permute-start(bf16[88,1408]{1,0:T(8,128)(2,1)} %param.13), channel_id=1, source_target_pairs={{0,8},{2,10},{4,12},{6,14},{8,0},{10,2},{12,4},{14,6},{16,24},{18,... | collective-permute-start | bytes 743432 | tf_op jit(solution)/shard_map/ppermute | solution.py:15
  19.4 30.4 %copy-start.47 = (f32[704]{0:T(1024)}, f32[704]{0:T(1024)S(1)}, u32[]{:S(2)}) copy-start(f32[704]{0:T(1024)S(1)} %get-tuple-element.67) | copy-start | bytes 8452
  19.4 30.4 %copy-start.49 = (f32[704]{0:T(1024)}, f32[704]{0:T(1024)S(1)}, u32[]{:S(2)}) copy-start(f32[704]{0:T(1024)S(1)} %get-tuple-element.68) | copy-start | bytes 8452
  19.4 30.4 %copy-start.51 = (f32[704]{0:T(1024)}, f32[704]{0:T(1024)S(1)}, u32[]{:S(2)}) copy-start(f32[704]{0:T(1024)S(1)} %get-tuple-element.69) | copy-start | bytes 8452
  19.4 30.4 %copy-start.53 = (f32[704]{0:T(1024)}, f32[704]{0:T(1024)S(1)}, u32[]{:S(2)}) copy-start(f32[704]{0:T(1024)S(1)} %get-tuple-element.70) | copy-start | bytes 8452
  19.4 30.4 %copy-start.55 = (f32[704]{0:T(1024)}, f32[704]{0:T(1024)S(1)}, u32[]{:S(2)}) copy-start(f32[704]{0:T(1024)S(1)} %get-tuple-element.71) | copy-start | bytes 8452
  19.4 30.4 %copy-start.57 = (f32[704]{0:T(1024)}, f32[704]{0:T(1024)S(1)}, u32[]{:S(2)}) copy-start(f32[704]{0:T(1024)S(1)} %get-tuple-element.72) | copy-start | bytes 8452
  19.4 30.4 %copy-start.59 = (f32[704]{0:T(1024)}, f32[704]{0:T(1024)S(1)}, u32[]{:S(2)}) copy-start(f32[704]{0:T(1024)S(1)} %get-tuple-element.73) | copy-start | bytes 8452
  19.4 30.4 %copy-start.61 = (f32[704]{0:T(1024)}, f32[704]{0:T(1024)S(1)}, u32[]{:S(2)}) copy-start(f32[704]{0:T(1024)S(1)} %get-tuple-element.74) | copy-start | bytes 8452
  19.4 30.4 %copy-start.63 = (f32[704]{0:T(1024)}, f32[704]{0:T(1024)S(1)}, u32[]{:S(2)}) copy-start(f32[704]{0:T(1024)S(1)} %get-tuple-element.75) | copy-start | bytes 8452
  19.4 30.4 %copy-start.65 = (f32[704]{0:T(1024)}, f32[704]{0:T(1024)S(1)}, u32[]{:S(2)}) copy-start(f32[704]{0:T(1024)S(1)} %get-tuple-element.76) | copy-start | bytes 8452
  19.5 30.4 %copy-start.67 = (f32[704]{0:T(1024)}, f32[704]{0:T(1024)S(1)}, u32[]{:S(2)}) copy-start(f32[704]{0:T(1024)S(1)} %get-tuple-element.77) | copy-start | bytes 8452
  19.5 30.4 %copy-start.69 = (f32[704]{0:T(1024)}, f32[704]{0:T(1024)S(1)}, u32[]{:S(2)}) copy-start(f32[704]{0:T(1024)S(1)} %get-tuple-element.78) | copy-start | bytes 8452
  19.5 30.4 %copy-start.71 = (f32[704]{0:T(1024)}, f32[704]{0:T(1024)S(1)}, u32[]{:S(2)}) copy-start(f32[704]{0:T(1024)S(1)} %get-tuple-element.79) | copy-start | bytes 8452
  19.5 30.4 %copy-start.73 = (f32[704]{0:T(1024)}, f32[704]{0:T(1024)S(1)}, u32[]{:S(2)}) copy-start(f32[704]{0:T(1024)S(1)} %get-tuple-element.80) | copy-start | bytes 8452
  19.5 30.4 %copy-start.75 = (f32[704]{0:T(1024)}, f32[704]{0:T(1024)S(1)}, u32[]{:S(2)}) copy-start(f32[704]{0:T(1024)S(1)} %get-tuple-element.81) | copy-start | bytes 8452
  19.5 30.4 %copy-start.77 = (f32[704]{0:T(1024)}, f32[704]{0:T(1024)S(1)}, u32[]{:S(2)}) copy-start(f32[704]{0:T(1024)S(1)} %get-tuple-element.82) | copy-start | bytes 8452
  19.5 30.4 %copy-start.79 = (f32[704]{0:T(1024)}, f32[704]{0:T(1024)S(1)}, u32[]{:S(2)}) copy-start(f32[704]{0:T(1024)S(1)} %get-tuple-element.83) | copy-start | bytes 8452
  19.5 30.4 %copy-start.81 = (f32[704]{0:T(1024)}, f32[704]{0:T(1024)S(1)}, u32[]{:S(2)}) copy-start(f32[704]{0:T(1024)S(1)} %get-tuple-element.84) | copy-start | bytes 8452
  19.5 30.4 %copy-start.83 = (f32[704]{0:T(1024)}, f32[704]{0:T(1024)S(1)}, u32[]{:S(2)}) copy-start(f32[704]{0:T(1024)S(1)} %get-tuple-element.85) | copy-start | bytes 8452
  19.7 30.3 %copy-start.85 = (f32[704]{0:T(1024)}, f32[704]{0:T(1024)S(1)}, u32[]{:S(2)}) copy-start(f32[704]{0:T(1024)S(1)} %get-tuple-element.105) | copy-start | bytes 8452
  19.7 30.3 %copy-start.87 = (f32[704]{0:T(1024)}, f32[704]{0:T(1024)S(1)}, u32[]{:S(2)}) copy-start(f32[704]{0:T(1024)S(1)} %get-tuple-element.106) | copy-start | bytes 8452
  19.7 30.3 %copy-start.89 = (f32[704]{0:T(1024)}, f32[704]{0:T(1024)S(1)}, u32[]{:S(2)}) copy-start(f32[704]{0:T(1024)S(1)} %get-tuple-element.107) | copy-start | bytes 8452
  21.2 15.1 %collective-permute-start.3 = (bf16[88,1408]{1,0:T(8,128)(2,1)S(1)}, bf16[88,1408]{1,0:T(8,128)(2,1)S(1)}, u32[]{:S(2)}, u32[]{:S(2)}) collective-permute-start(bf16[88,1408]{1,0:T(8,128)(2,1)S(1)} %copy-done.9), channel_id=1, source_target_pairs={{0,16},{2,18},{4,20},{6,22},{8,24},{10,26},{12,28},{14,30},{16,0},... | collective-permute-start | bytes 743432 | tf_op jit(solution)/shard_map/ppermute | solution.py:15
  22.3 14.7 %collective-permute-start = (bf16[3,64,704]{2,1,0:T(8,128)(2,1)S(1)}, bf16[3,64,704]{2,1,0:T(8,128)(2,1)S(1)}, u32[]{:S(2)}, u32[]{:S(2)}) collective-permute-start(bf16[3,64,704]{2,1,0:T(8,128)(2,1)S(1)} %get-tuple-element.127), channel_id=1, source_target_pairs={{0,2},{2,4},{4,6},{6,8},{8,10},{10,12},{12,14},{14,16},{16,18},{18... | collective-permute-start | bytes 811016 | tf_op jit(solution)/shard_map/ppermute | solution.py:26
  25.4 14.6 %collective-permute-start.1 = (bf16[3,64,704]{2,1,0:T(8,128)(2,1)S(1)}, bf16[3,64,704]{2,1,0:T(8,128)(2,1)S(1)}, u32[]{:S(2)}, u32[]{:S(2)}) collective-permute-start(bf16[3,64,704]{2,1,0:T(8,128)(2,1)S(1)} %get-tuple-element.128), channel_id=1, source_target_pairs={{2,0},{4,2},{6,4},{8,6},{10,8},{12,10},{14,12},{16,14},{18,16},{20... | collective-permute-start | bytes 811016 | tf_op jit(solution)/shard_map/ppermute | solution.py:27
  36.2 34.5 %collective-permute-start.5 = (bf16[88,1408]{1,0:T(8,128)(2,1)S(1)}, bf16[88,1408]{1,0:T(8,128)(2,1)}, u32[]{:S(2)}, u32[]{:S(2)}) collective-permute-start(bf16[88,1408]{1,0:T(8,128)(2,1)S(1)} %copy-done.9), channel_id=1, source_target_pairs={{0,4},{2,6},{4,0},{6,2},{8,12},{10,14},{12,8},{14,10},{16,20},{18,... | collective-permute-start | bytes 743432 | tf_op jit(solution)/shard_map/ppermute | solution.py:15
  37.0 35.5 %collective-permute-start.6 = (bf16[88,1408]{1,0:T(8,128)(2,1)S(1)}, bf16[88,1408]{1,0:T(8,128)(2,1)}, u32[]{:S(2)}, u32[]{:S(2)}) collective-permute-start(bf16[88,1408]{1,0:T(8,128)(2,1)S(1)} %copy-done.9), channel_id=1, source_target_pairs={{0,2},{2,0},{4,6},{6,4},{8,10},{10,8},{12,14},{14,12},{16,18},{18,... | collective-permute-start | bytes 743432 | tf_op jit(solution)/shard_map/ppermute | solution.py:15
  40.0 16.9 %collective-permute-start.19 = (bf16[88,1408]{1,0:T(8,128)(2,1)S(1)}, bf16[88,1408]{1,0:T(8,128)(2,1)S(1)}, u32[]{:S(2)}, u32[]{:S(2)}) collective-permute-start(bf16[88,1408]{1,0:T(8,128)(2,1)S(1)} %collective-permute-done.18), channel_id=1, source_target_pairs={{0,8},{2,10},{4,12},{6,14},{8,0},{10,2},{12,4},{14,6},{16,24},{18,... | collective-permute-start | bytes 743432 | tf_op jit(solution)/shard_map/ppermute | solution.py:15
  56.8 8.1 %collective-permute-start.4 = (bf16[88,1408]{1,0:T(8,128)(2,1)S(1)}, bf16[88,1408]{1,0:T(8,128)(2,1)S(1)}, u32[]{:S(2)}, u32[]{:S(2)}) collective-permute-start(bf16[88,1408]{1,0:T(8,128)(2,1)S(1)} %collective-permute-done.3), channel_id=1, source_target_pairs={{0,8},{2,10},{4,12},{6,14},{8,0},{10,2},{12,4},{14,6},{16,24},{18,... | collective-permute-start | bytes 743432 | tf_op jit(solution)/shard_map/ppermute | solution.py:15
  56.9 19.2 %collective-permute-start.22 = (bf16[88,1408]{1,0:T(8,128)(2,1)}, bf16[88,1408]{1,0:T(8,128)(2,1)S(1)}, u32[]{:S(2)}, u32[]{:S(2)}) collective-permute-start(bf16[88,1408]{1,0:T(8,128)(2,1)} %collective-permute-done.20), channel_id=1, source_target_pairs={{0,4},{2,6},{4,0},{6,2},{8,12},{10,14},{12,8},{14,10},{16,20},{18,... | collective-permute-start | bytes 743432 | tf_op jit(solution)/shard_map/ppermute | solution.py:15
  64.8 20.4 %collective-permute-start.23 = (bf16[88,1408]{1,0:T(8,128)(2,1)S(1)}, bf16[88,1408]{1,0:T(8,128)(2,1)S(1)}, u32[]{:S(2)}, u32[]{:S(2)}) collective-permute-start(bf16[88,1408]{1,0:T(8,128)(2,1)S(1)} %collective-permute-done.17), channel_id=1, source_target_pairs={{0,2},{2,0},{4,6},{6,4},{8,10},{10,8},{12,14},{14,12},{16,18},{18,... | collective-permute-start | bytes 743432 | tf_op jit(solution)/shard_map/ppermute | solution.py:15
  65.6 22.1 %collective-permute-start.24 = (bf16[88,1408]{1,0:T(8,128)(2,1)S(1)}, bf16[88,1408]{1,0:T(8,128)(2,1)S(1)}, u32[]{:S(2)}, u32[]{:S(2)}) collective-permute-start(bf16[88,1408]{1,0:T(8,128)(2,1)S(1)} %collective-permute-done.17), channel_id=1, source_target_pairs={{0,4},{2,6},{4,0},{6,2},{8,12},{10,14},{12,8},{14,10},{16,20},{18,... | collective-permute-start | bytes 743432 | tf_op jit(solution)/shard_map/ppermute | solution.py:15
  70.8 25.8 %collective-permute-start.26 = (bf16[88,1408]{1,0:T(8,128)(2,1)S(1)}, bf16[88,1408]{1,0:T(8,128)(2,1)S(1)}, u32[]{:S(2)}, u32[]{:S(2)}) collective-permute-start(bf16[88,1408]{1,0:T(8,128)(2,1)S(1)} %collective-permute-done.18), channel_id=1, source_target_pairs={{0,2},{2,0},{4,6},{6,4},{8,10},{10,8},{12,14},{14,12},{16,18},{18,... | collective-permute-start | bytes 743432 | tf_op jit(solution)/shard_map/ppermute | solution.py:15
  72.4 10.3 %collective-permute-start.7 = (bf16[88,1408]{1,0:T(8,128)(2,1)}, bf16[88,1408]{1,0:T(8,128)(2,1)S(1)}, u32[]{:S(2)}, u32[]{:S(2)}) collective-permute-start(bf16[88,1408]{1,0:T(8,128)(2,1)} %collective-permute-done.5), channel_id=1, source_target_pairs={{0,2},{2,0},{4,6},{6,4},{8,10},{10,8},{12,14},{14,12},{16,18},{18,... | collective-permute-start | bytes 743432 | tf_op jit(solution)/shard_map/ppermute | solution.py:15
  76.1 30.3 %collective-permute-start.27 = (bf16[88,1408]{1,0:T(8,128)(2,1)S(1)}, bf16[88,1408]{1,0:T(8,128)(2,1)S(1)}, u32[]{:S(2)}, u32[]{:S(2)}) collective-permute-start(bf16[88,1408]{1,0:T(8,128)(2,1)S(1)} %collective-permute-done.18), channel_id=1, source_target_pairs={{0,4},{2,6},{4,0},{6,2},{8,12},{10,14},{12,8},{14,10},{16,20},{18,... | collective-permute-start | bytes 743432 | tf_op jit(solution)/shard_map/ppermute | solution.py:15
  82.8 8.2 %collective-permute-start.8 = (bf16[88,1408]{1,0:T(8,128)(2,1)S(1)}, bf16[88,1408]{1,0:T(8,128)(2,1)S(1)}, u32[]{:S(2)}, u32[]{:S(2)}) collective-permute-start(bf16[88,1408]{1,0:T(8,128)(2,1)S(1)} %collective-permute-done.2), channel_id=1, source_target_pairs={{0,4},{2,6},{4,0},{6,2},{8,12},{10,14},{12,8},{14,10},{16,20},{18,... | collective-permute-start | bytes 743432 | tf_op jit(solution)/shard_map/ppermute | solution.py:15
  85.2 8.9 %collective-permute-start.9 = (bf16[88,1408]{1,0:T(8,128)(2,1)S(1)}, bf16[88,1408]{1,0:T(8,128)(2,1)S(1)}, u32[]{:S(2)}, u32[]{:S(2)}) collective-permute-start(bf16[88,1408]{1,0:T(8,128)(2,1)S(1)} %collective-permute-done.2), channel_id=1, source_target_pairs={{0,2},{2,0},{4,6},{6,4},{8,10},{10,8},{12,14},{14,12},{16,18},{18,... | collective-permute-start | bytes 743432 | tf_op jit(solution)/shard_map/ppermute | solution.py:15
  87.7 18.0 %collective-permute-start.11 = (bf16[88,1408]{1,0:T(8,128)(2,1)S(1)}, bf16[88,1408]{1,0:T(8,128)(2,1)S(1)}, u32[]{:S(2)}, u32[]{:S(2)}) collective-permute-start(bf16[88,1408]{1,0:T(8,128)(2,1)S(1)} %collective-permute-done.3), channel_id=1, source_target_pairs={{0,4},{2,6},{4,0},{6,2},{8,12},{10,14},{12,8},{14,10},{16,20},{18,... | collective-permute-start | bytes 743432 | tf_op jit(solution)/shard_map/ppermute | solution.py:15
  88.4 38.0 %copy-start = (bf16[256,1408]{1,0:T(8,128)(2,1)S(1)}, bf16[256,1408]{1,0:T(8,128)(2,1)}, u32[]{:S(2)}) copy-start(bf16[256,1408]{1,0:T(8,128)(2,1)} %copy.15.scaled) | copy-start | bytes 2162692
  88.4 38.0 %copy-start.1 = (bf16[256,1408]{1,0:T(8,128)(2,1)S(1)}, bf16[256,1408]{1,0:T(8,128)(2,1)}, u32[]{:S(2)}) copy-start(bf16[256,1408]{1,0:T(8,128)(2,1)} %copy.14.normed) | copy-start | bytes 2162692
  91.0 9.0 %collective-permute-start.25 = (bf16[88,1408]{1,0:T(8,128)(2,1)S(1)}, bf16[88,1408]{1,0:T(8,128)(2,1)S(1)}, u32[]{:S(2)}, u32[]{:S(2)}) collective-permute-start(bf16[88,1408]{1,0:T(8,128)(2,1)S(1)} %collective-permute-done.23), channel_id=1, source_target_pairs={{0,4},{2,6},{4,0},{6,2},{8,12},{10,14},{12,8},{14,10},{16,20},{18,... | collective-permute-start | bytes 743432 | tf_op jit(solution)/shard_map/ppermute | solution.py:15
  94.2 20.5 %collective-permute-start.12 = (bf16[88,1408]{1,0:T(8,128)(2,1)S(1)}, bf16[88,1408]{1,0:T(8,128)(2,1)S(1)}, u32[]{:S(2)}, u32[]{:S(2)}) collective-permute-start(bf16[88,1408]{1,0:T(8,128)(2,1)S(1)} %collective-permute-done.3), channel_id=1, source_target_pairs={{0,2},{2,0},{4,6},{6,4},{8,10},{10,8},{12,14},{14,12},{16,18},{18,... | collective-permute-start | bytes 743432 | tf_op jit(solution)/shard_map/ppermute | solution.py:15
  96.6 6.6 %collective-permute-start.10 = (bf16[88,1408]{1,0:T(8,128)(2,1)S(1)}, bf16[88,1408]{1,0:T(8,128)(2,1)S(1)}, u32[]{:S(2)}, u32[]{:S(2)}) collective-permute-start(bf16[88,1408]{1,0:T(8,128)(2,1)S(1)} %collective-permute-done.8), channel_id=1, source_target_pairs={{0,2},{2,0},{4,6},{6,4},{8,10},{10,8},{12,14},{14,12},{16,18},{18,... | collective-permute-start | bytes 743432 | tf_op jit(solution)/shard_map/ppermute | solution.py:15
  100.0 7.9 %collective-permute-start.28 = (bf16[88,1408]{1,0:T(8,128)(2,1)S(1)}, bf16[88,1408]{1,0:T(8,128)(2,1)S(1)}, u32[]{:S(2)}, u32[]{:S(2)}) collective-permute-start(bf16[88,1408]{1,0:T(8,128)(2,1)S(1)} %collective-permute-done.26), channel_id=1, source_target_pairs={{0,4},{2,6},{4,0},{6,2},{8,12},{10,14},{12,8},{14,10},{16,20},{18,... | collective-permute-start | bytes 743432 | tf_op jit(solution)/shard_map/ppermute | solution.py:15
  103.2 8.8 %collective-permute-start.29 = (bf16[88,1408]{1,0:T(8,128)(2,1)S(1)}, bf16[88,1408]{1,0:T(8,128)(2,1)S(1)}, u32[]{:S(2)}, u32[]{:S(2)}) collective-permute-start(bf16[88,1408]{1,0:T(8,128)(2,1)S(1)} %collective-permute-done.19), channel_id=1, source_target_pairs={{0,2},{2,0},{4,6},{6,4},{8,10},{10,8},{12,14},{14,12},{16,18},{18,... | collective-permute-start | bytes 743432 | tf_op jit(solution)/shard_map/ppermute | solution.py:15
  105.7 16.6 %collective-permute-start.30 = (bf16[88,1408]{1,0:T(8,128)(2,1)S(1)}, bf16[88,1408]{1,0:T(8,128)(2,1)S(1)}, u32[]{:S(2)}, u32[]{:S(2)}) collective-permute-start(bf16[88,1408]{1,0:T(8,128)(2,1)S(1)} %collective-permute-done.19), channel_id=1, source_target_pairs={{0,4},{2,6},{4,0},{6,2},{8,12},{10,14},{12,8},{14,10},{16,20},{18,... | collective-permute-start | bytes 743432 | tf_op jit(solution)/shard_map/ppermute | solution.py:15
  106.5 14.5 %collective-permute-start.13 = (bf16[88,1408]{1,0:T(8,128)(2,1)S(1)}, bf16[88,1408]{1,0:T(8,128)(2,1)S(1)}, u32[]{:S(2)}, u32[]{:S(2)}) collective-permute-start(bf16[88,1408]{1,0:T(8,128)(2,1)S(1)} %collective-permute-done.11), channel_id=1, source_target_pairs={{0,2},{2,0},{4,6},{6,4},{8,10},{10,8},{12,14},{14,12},{16,18},{18,... | collective-permute-start | bytes 743432 | tf_op jit(solution)/shard_map/ppermute | solution.py:15
  107.9 11.6 %collective-permute-start.14 = (bf16[88,1408]{1,0:T(8,128)(2,1)S(1)}, bf16[88,1408]{1,0:T(8,128)(2,1)S(1)}, u32[]{:S(2)}, u32[]{:S(2)}) collective-permute-start(bf16[88,1408]{1,0:T(8,128)(2,1)S(1)} %collective-permute-done.4), channel_id=1, source_target_pairs={{0,4},{2,6},{4,0},{6,2},{8,12},{10,14},{12,8},{14,10},{16,20},{18,... | collective-permute-start | bytes 743432 | tf_op jit(solution)/shard_map/ppermute | solution.py:15
  112.0 11.1 %collective-permute-start.15 = (bf16[88,1408]{1,0:T(8,128)(2,1)S(1)}, bf16[88,1408]{1,0:T(8,128)(2,1)S(1)}, u32[]{:S(2)}, u32[]{:S(2)}) collective-permute-start(bf16[88,1408]{1,0:T(8,128)(2,1)S(1)} %collective-permute-done.4), channel_id=1, source_target_pairs={{0,2},{2,0},{4,6},{6,4},{8,10},{10,8},{12,14},{14,12},{16,18},{18,... | collective-permute-start | bytes 743432 | tf_op jit(solution)/shard_map/ppermute | solution.py:15
  114.7 9.1 %collective-permute-start.31 = (bf16[88,1408]{1,0:T(8,128)(2,1)S(1)}, bf16[88,1408]{1,0:T(8,128)(2,1)S(1)}, u32[]{:S(2)}, u32[]{:S(2)}) collective-permute-start(bf16[88,1408]{1,0:T(8,128)(2,1)S(1)} %collective-permute-done.29), channel_id=1, source_target_pairs={{0,4},{2,6},{4,0},{6,2},{8,12},{10,14},{12,8},{14,10},{16,20},{18,... | collective-permute-start | bytes 743432 | tf_op jit(solution)/shard_map/ppermute | solution.py:15
  119.5 6.2 %collective-permute-start.16 = (bf16[88,1408]{1,0:T(8,128)(2,1)S(1)}, bf16[88,1408]{1,0:T(8,128)(2,1)S(1)}, u32[]{:S(2)}, u32[]{:S(2)}) collective-permute-start(bf16[88,1408]{1,0:T(8,128)(2,1)S(1)} %collective-permute-done.14), channel_id=1, source_target_pairs={{0,2},{2,0},{4,6},{6,4},{8,10},{10,8},{12,14},{14,12},{16,18},{18,... | collective-permute-start | bytes 743432 | tf_op jit(solution)/shard_map/ppermute | solution.py:15
  135.9 2.5 %collective-permute-start.33 = (f32[256,704]{0,1:T(8,128)}, f32[256,704]{0,1:T(8,128)}, u32[]{:S(2)}, u32[]{:S(2)}) collective-permute-start(f32[256,704]{0,1:T(8,128)} %copy.18), channel_id=1, source_target_pairs={{0,1},{1,0},{2,3},{3,2},{4,5},{5,4},{6,7},{7,6},{8,9},{9,8},{10,11... | collective-permute-start | bytes 2162696 | tf_op jit(solution)/shard_map/ppermute | solution.py:19
  137.1 28.0 %collective-permute-start.32 = (f32[256,704]{0,1:T(8,128)}, f32[256,704]{0,1:T(8,128)}, u32[]{:S(2)}, u32[]{:S(2)}) collective-permute-start(f32[256,704]{0,1:T(8,128)} %copy.16), channel_id=1, source_target_pairs={{0,1},{1,0},{2,3},{3,2},{4,5},{5,4},{6,7},{7,6},{8,9},{9,8},{10,11... | collective-permute-start | bytes 2162696 | tf_op jit(solution)/shard_map/ppermute | solution.py:19
  169.0 6.5 %collective-permute-start.36 = (f32[52,704]{1,0:T(8,128)S(1)}, f32[52,704]{1,0:T(8,128)S(1)}, u32[]{:S(2)}, u32[]{:S(2)}) collective-permute-start(f32[52,704]{1,0:T(8,128)S(1)} %stack.211), channel_id=1, source_target_pairs={{0,2},{2,0},{4,6},{6,4},{8,10},{10,8},{12,14},{14,12},{16,18},{18,... | collective-permute-start | bytes 439304 | tf_op jit(solution)/shard_map/ppermute | solution.py:15
  170.3 16.1 %collective-permute-start.34 = (bf16[3,64,704]{2,1,0:T(8,128)(2,1)S(1)}, bf16[3,64,704]{2,1,0:T(8,128)(2,1)S(1)}, u32[]{:S(2)}, u32[]{:S(2)}) collective-permute-start(bf16[3,64,704]{2,1,0:T(8,128)(2,1)S(1)} %get-tuple-element.125), channel_id=1, source_target_pairs={{0,2},{2,4},{4,6},{6,8},{8,10},{10,12},{12,14},{14,16},{16,18},{18... | collective-permute-start | bytes 811016 | tf_op jit(solution)/shard_map/ppermute | solution.py:26
  173.5 15.4 %collective-permute-start.35 = (bf16[3,64,704]{2,1,0:T(8,128)(2,1)S(1)}, bf16[3,64,704]{2,1,0:T(8,128)(2,1)S(1)}, u32[]{:S(2)}, u32[]{:S(2)}) collective-permute-start(bf16[3,64,704]{2,1,0:T(8,128)(2,1)S(1)} %get-tuple-element.126), channel_id=1, source_target_pairs={{2,0},{4,2},{6,4},{8,6},{10,8},{12,10},{14,12},{16,14},{18,16},{20... | collective-permute-start | bytes 811016 | tf_op jit(solution)/shard_map/ppermute | solution.py:27
  175.5 13.4 %collective-permute-start.37 = (f32[52,704]{1,0:T(8,128)S(1)}, f32[52,704]{1,0:T(8,128)S(1)}, u32[]{:S(2)}, u32[]{:S(2)}) collective-permute-start(f32[52,704]{1,0:T(8,128)S(1)} %add.528), channel_id=1, source_target_pairs={{0,4},{2,6},{4,0},{6,2},{8,12},{10,14},{12,8},{14,10},{16,20},{18,... | collective-permute-start | bytes 439304 | tf_op jit(solution)/shard_map/ppermute | solution.py:15
  189.0 5.5 %collective-permute-start.38 = (f32[52,704]{1,0:T(8,128)S(1)}, f32[52,704]{1,0:T(8,128)S(1)}, u32[]{:S(2)}, u32[]{:S(2)}) collective-permute-start(f32[52,704]{1,0:T(8,128)S(1)} %add.529), channel_id=1, source_target_pairs={{0,8},{2,10},{4,12},{6,14},{8,0},{10,2},{12,4},{14,6},{16,24},{18,... | collective-permute-start | bytes 439304 | tf_op jit(solution)/shard_map/ppermute | solution.py:15
  194.5 11.5 %collective-permute-start.39 = (f32[52,704]{1,0:T(8,128)S(1)}, f32[52,704]{1,0:T(8,128)S(1)}, u32[]{:S(2)}, u32[]{:S(2)}) collective-permute-start(f32[52,704]{1,0:T(8,128)S(1)} %add.530), channel_id=1, source_target_pairs={{0,16},{2,18},{4,20},{6,22},{8,24},{10,26},{12,28},{14,30},{16,0},... | collective-permute-start | bytes 439304 | tf_op jit(solution)/shard_map/ppermute | solution.py:15
  (99 other events, 2029.6 us)
